TPU v7x, 256 devices: a whole 4x4x8 slice. The times are simulated.
256 devices in a mesh: sec: 8 (over x, core), term: 32 (over y, z).
Axes of the slice: x: 4, y: 4, z: 8, core: 2. Of those that a mesh axis runs over, the one named last changes fastest.
Arguments:
- env_blocks: bfloat16 [32, 16, 256, 256], P('term', 'sec'), may hold values from -6 to 6
- core_blocks: bfloat16 [512, 256, 256], P('sec', 'term'), may hold values from -0.375 to 0.375
- mpo_coeffs: bfloat16 [32, 32, 512], P(None, None, 'sec'), may hold values from -1 to 1
- pair_left: int32 [512], P('sec'), may hold values from 0 to 1
- pair_right: int32 [512], P('sec'), may hold values from 0 to 15
- block_dims: int32 [16], replicated, may hold values from 1 to 256, 3072 in all
Outputs:
- new_env: float32 [32, 16, 256, 256], P('term', 'sec')
Inputs may be any that keep to these rules, and one draw needn't show every extreme that they name: `pair_left`: A pair's left block is one of the 2 blocks of the sec index that holds the pair.
All inputs are finite; a program needn't handle non-finite values.
Results may differ from a plain program's by a relative error of at most 0.004.
Values may be sent and summed in bfloat16 or wider, within the bound.
A program may use at most 128 MiB of HBM per device.

v0:
```python
import jax
import jax.numpy as jnp
from jax import lax
from jax.sharding import PartitionSpec as P


def split_up(array, dim, peers):
    before, after = (array.shape[:dim], array.shape[dim + 1 :])
    return jnp.moveaxis(array.reshape(*before, peers, -1, *after), dim, 0)


def sum_at_owner(array, axis, dim):
    peers = lax.axis_size(axis)
    pieces = lax.all_to_all(split_up(array, dim, peers), axis, 0, 0, tiled=True)
    return jnp.sum(pieces, axis=0)


def per_device(env_blocks, core_blocks, mpo_coeffs, pair_left, pair_right, block_dims):
    nb_local = env_blocks.shape[1]
    blk = env_blocks.shape[2]
    pairs_local = core_blocks.shape[0]
    total_blocks = block_dims.shape[0]
    sec_index = lax.axis_index("sec")
    term_index = lax.axis_index("term")
    core_full = lax.all_gather(core_blocks, "term", axis=1, tiled=True)
    block_ids = jnp.arange(total_blocks)
    left_global = sec_index * nb_local + pair_left
    dims_left = jnp.sum(
        jnp.where(left_global[:, None] == block_ids[None, :], block_dims[None, :], 0), axis=1
    )
    right_match = pair_right[:, None] == block_ids[None, :]
    dims_right = jnp.sum(jnp.where(right_match, block_dims[None, :], 0), axis=1)
    rows = jnp.arange(blk)
    keep = (rows[None, :, None] < dims_left[:, None, None]) & (
        rows[None, None, :] < dims_right[:, None, None]
    )
    masked = jnp.where(keep, core_full, jnp.zeros((), core_full.dtype))
    left_onehot = (pair_left[:, None] == jnp.arange(nb_local)[None, :]).astype(jnp.bfloat16)
    own_coeffs = lax.dynamic_index_in_dim(mpo_coeffs, term_index, 1, keepdims=False)
    piece = lax.all_gather(env_blocks, "term", axis=0, tiled=True)
    count = piece.shape[0]
    weights = own_coeffs[:, :, None] * left_onehot[None, :, :]
    flat = piece.reshape(count, nb_local, blk * blk)
    summed_terms = jnp.einsum("wpi,wix->px", weights, flat, preferred_element_type=jnp.float32)
    mixed = summed_terms.astype(jnp.bfloat16).reshape(pairs_local, blk, blk)
    half = jnp.einsum("prc,pcd->prd", mixed, masked, preferred_element_type=jnp.float32).astype(
        jnp.bfloat16
    )
    pair_terms = jnp.einsum("prc,prd->pcd", masked, half, preferred_element_type=jnp.float32)
    pair_terms = pair_terms.reshape(pairs_local, blk * blk)
    right_onehot = right_match.astype(jnp.float32)
    owned = sum_at_owner(
        jnp.dot(
            right_onehot.T,
            pair_terms,
            precision=lax.Precision.HIGHEST,
            preferred_element_type=jnp.float32,
        ),
        "sec",
        0,
    )
    return owned.reshape(1, nb_local, blk, blk)


def solution(mesh):
    return jax.shard_map(
        per_device,
        mesh=mesh,
        in_specs=(
            P("term", "sec", None, None),
            P("sec", "term", None),
            P(None, None, "sec"),
            P("sec"),
            P("sec"),
            P(),
        ),
        out_specs=P("term", "sec", None, None),
        check_vma=False,
    )
```

profile of v0, /device:TPU:1, one launch (start us, length us, event | category | flops | bytes accessed | tf_op | source)
XLA Modules:
  0.0 324.6 jit_solution(13647272893543834493)
XLA Ops:
  6.5 0.0 copy-start
  6.5 0.0 all-gather.5.cloned.1.call-start
  6.5 0.7 all-gather.5.cloned.1.call-update
  7.3 0.0 all-gather.3.cloned.1.call-start
  7.3 0.7 all-gather.3.cloned.1.call-update
  8.0 0.0 copy-done
  8.1 0.7 broadcast_add_fusion
  8.7 0.8 select_reduce_fusion.1
  9.5 0.7 compare_convert_fusion
  10.2 0.1 iota_compare_fusion
  10.3 100.6 %all-gather.5.cloned.1.call-done = bf16[32,2,256,256]{3,2,1,0:T(8,128)(2,1)} async-done(((bf16[1,2,256,256]{3,2,1,0:T(8,128)(2,1)}), bf16[32,2,256,256]{3,2,1,0:T(8,128)(2,1)}) %all-gather.5.cloned.1.call-update) | async-done | bytes 8388624 | tf_op jit(solution)/shard_map/all_gather | solution.py:40
  110.9 19.8 %reshape.106 = bf16[32,2,65536]{2,1,0:T(2,128)(2,1)} reshape(bf16[32,2,256,256]{3,2,1,0:T(8,128)(2,1)} %all-gather.5.cloned.1.call-done) | data formatting | bytes 16777216 | tf_op jit(solution)/shard_map/reshape | solution.py:43
  130.7 13.2 %fusion = bf16[64,65536]{1,0:T(8,128)(2,1)} fusion(bf16[32,2,65536]{2,1,0:T(2,128)(2,1)} %reshape.106, bf16[64,2]{0,1:T(2,128)(2,1)S(1)} %compare_convert_fusion, bf16[32,64]{1,0:T(8,128)(2,1)S(1)} %bitcast.26), kind=kOutput, calls=%fused_computation.1 | convolution fusion | flops 541069312 | bytes 16781568 | tf_op jit(solution)/shard_map/wpi,wix->px/dot_general | solution.py:44
  143.8 8.9 %copy.23 = bf16[8,8,256,256]{3,2,1,0:T(8,128)(2,1)} copy(bf16[8,8,256,256]{3,1,2,0:T(8,128)(2,1)} %bitcast.23) | data formatting | bytes 16777216
  152.7 57.5 %all-gather.3.cloned.1.call-done = bf16[64,256,256]{2,1,0:T(8,128)(2,1)} async-done(((bf16[64,8,256]{2,1,0:T(8,128)(2,1)}), bf16[64,256,256]{2,1,0:T(8,128)(2,1)}) %all-gather.3.cloned.1.call-update) | async-done | bytes 8388624 | tf_op jit(solution)/shard_map/all_gather | solution.py:25
  210.3 0.0 copy-start.2
  210.3 9.4 %fusion.30 = bf16[64,256,256]{2,1,0:T(8,128)(2,1)S(1)} fusion(bf16[64,256,256]{2,1,0:T(8,128)(2,1)} %bitcast.24, bf16[64,256,256]{2,1,0:T(8,128)(2,1)} %all-gather.3.cloned.1.call-done, pred[64,256]{1,0:T(8,128)(4,1)S(1)} %get-tuple-element.7, pred[64,256]{1,0:T(8,128)(4,1)S(1)} %get-tuple-element.8), kind=kOutput, calls=%fused_computation.5.clone.2 | convolution fusion | flops 2160066560 | bytes 25198592 | tf_op jit(solution)/shard_map/prc,pcd->prd/dot_general | solution.py:46
  219.6 0.0 copy-done.2
  219.6 9.8 %fusion.2 = f32[64,256,256]{2,1,0:T(8,128)} fusion(bf16[64,256,256]{2,1,0:T(8,128)(2,1)S(1)} %copy-done.2, pred[64,256]{1,0:T(8,128)(4,1)S(1)} %get-tuple-element.7, pred[64,256]{1,0:T(8,128)(4,1)S(1)} %get-tuple-element.8, bf16[64,256,256]{2,1,0:T(8,128)(2,1)S(1)} %fusion.30), kind=kOutput, calls=%fused_computation.4 | convolution fusion | flops 2155872256 | bytes 33587200 | tf_op jit(solution)/shard_map/prc,prd->pcd/dot_general | solution.py:49
  229.4 0.0 copy-start.3
  229.4 14.5 %reshape.105 = f32[64,65536,1]{1,0,2:T(8,128)} reshape(f32[64,256,256]{2,1,0:T(8,128)} %fusion.2) | data formatting | bytes 33554432 | tf_op jit(solution)/shard_map/reshape | solution.py:50
  243.9 0.0 copy-done.3
  243.9 9.3 %fusion.15 = f32[8,2,65536]{2,0,1:T(8,128)S(1)} fusion(f32[64,65536,1]{1,0,2:T(8,128)} %reshape.105, s32[8,2]{0,1:T(2,128)S(1)} %multiply_add_fusion, s32[64]{0:T(128)S(1)} %copy-done.3), kind=kOutput, calls=%fused_computation.21 | convolution fusion | flops 805307392 | bytes 20971840 | tf_op jit(solution)/shard_map/dot_general | solution.py:53
  253.3 0.0 copy-start.1
  253.3 3.2 copy.19
  256.6 56.7 %all_to_all.5 = f32[8,2,65536]{2,1,0:T(2,128)} all-to-all(f32[8,2,65536]{2,1,0:T(2,128)S(1)} %copy.19), channel_id=1, replica_groups=mesh['sec'=8,'term'=32] {'sec'}, dimensions={0} | all-to-all | bytes 8388608 | tf_op jit(solution)/shard_map/all_to_all | solution.py:14
  313.2 3.7 %reduce_sum.29 = f32[2,65536]{1,0:T(2,128)S(1)} reduce(f32[8,2,65536]{2,1,0:T(2,128)} %all_to_all.5, f32[]{:T(128)} %constant.22.clone.1), dimensions={0}, to_apply=%region_2.3 | reduce | flops 917504 | bytes 4718596 | tf_op jit(solution)/shard_map/reduce_sum | solution.py:15
  317.0 0.8 copy.29
  317.8 0.0 copy-done.1
  (3 shorter events, 0.0 us)
Async XLA Ops:
  6.5 1.5 copy-start
  6.5 104.3 %all-gather.5.cloned.1.call-start = ((), (), s32[]{:S(2)}) async-start(), calls=%async_computation.2 | async-start | bytes 8650752 | tf_op jit(solution)/shard_map/all_gather | solution.py:40
  7.3 203.0 %all-gather.3.cloned.1.call-start = ((), (), s32[]{:S(2)}) async-start(), calls=%async_computation.1 | async-start | bytes 8650752 | tf_op jit(solution)/shard_map/all_gather | solution.py:25
  210.3 9.4 %copy-start.2 = (bf16[64,256,256]{2,1,0:T(8,128)(2,1)S(1)}, bf16[64,256,256]{2,1,0:T(8,128)(2,1)}, u32[]{:S(2)}) copy-start(bf16[64,256,256]{2,1,0:T(8,128)(2,1)} %all-gather.3.cloned.1.call-done) | copy-start | bytes 25165828
  229.4 14.5 %copy-start.3 = (s32[64]{0:T(128)S(1)}, s32[64]{0:T(128)}, u32[]{:S(2)}) copy-start(s32[64]{0:T(128)} %param.10) | copy-start | bytes 772
  253.3 64.5 %copy-start.1 = (bf16[32,32,64]{2,1,0:T(8,128)(2,1)S(1)}, bf16[32,32,64]{2,1,0:T(8,128)(2,1)}, u32[]{:S(2)}) copy-start(bf16[32,32,64]{2,1,0:T(8,128)(2,1)} %param.8) | copy-start | bytes 393220
Sparse Core Ops, SparseCore 0:
  9.9 100.9 all-gather.4
  113.3 96.8 all-gather.2
where the time goes:
time: 326 us; the launch traced here: 325 us
  waiting for transfers between devices  160 us (49%)
  blocking collectives  56.7 us (17%)
  local copies, waits for them, and re-layouts  47.3 us (15%)
  matrix products  41.6 us (13%)
  between operations  13.5 us (4%)
  other arithmetic  5.9 us (2%)
    all_gather x1, waiting for transfers between devices, per_device(): piece = lax.all_gather(env_blocks, 'term', axis=0, tiled=True)  101 us
    all_gather x1, waiting for transfers between devices, per_device(): core_full = lax.all_gather(core_blocks, 'term', axis=1, tiled=True)  57.5 us
    all_to_all x1, blocking collectives, sum_at_owner(): pieces = lax.all_to_all(split_up(array, dim, peers), axis, 0, 0, tiled=True)  56.7 us
    reshape x1, local copies, waits for them, and re-layouts, per_device(): flat = piece.reshape(count, nb_local, blk * blk)  19.8 us
    reshape x1, local copies, waits for them, and re-layouts, per_device(): pair_terms = pair_terms.reshape(pairs_local, blk * blk)  14.5 us
    dot_general x1, matrix products, per_device(): jnp.einsum('wpi,wix->px', weights, flat, preferred_element_type=jnp.float32)  13.2 us
    dot_general x1, matrix products, per_device(): jnp.einsum('prc,prd->pcd', masked, half, preferred_element_type=jnp.float32)  9.76 us
    unnamed x11, local copies, waits for them, and re-layouts  9.72 us
  transfers between devices with their start and end apart: 2, of which 2 were waited for; matrix products, arithmetic and copies ran while one was open for 14% of the time, Pallas kernels for 0%

commit v1 on v0

--- a/solution.py
+++ b/solution.py
@@ -2,6 +2,13 @@
 import jax.numpy as jnp
 from jax import lax
 from jax.sharding import PartitionSpec as P
+
+
+def _draw_threads(w_in):
+    everything = tuple((w_in for _ in range(lax.axis_size("term"))))
+    h_now = jnp.stack(everything)
+    res = lax.all_to_all(h_now, "term", 0, 0)
+    return jnp.concatenate(res, axis=1)
 
 
 def split_up(array, dim, peers):
@@ -22,7 +29,7 @@
     total_blocks = block_dims.shape[0]
     sec_index = lax.axis_index("sec")
     term_index = lax.axis_index("term")
-    core_full = lax.all_gather(core_blocks, "term", axis=1, tiled=True)
+    core_full = _draw_threads(core_blocks)
     block_ids = jnp.arange(total_blocks)
     left_global = sec_index * nb_local + pair_left
     dims_left = jnp.sum(

time: 326 us -> 409 us (1.25)
  waiting for transfers between devices: 160 us -> 229 us
  starting transfers between devices: 0.04 us -> 12.3 us
  local copies, waits for them, and re-layouts: 47.3 us -> 52.3 us
    all_gather x1, waiting for transfers between devices: 101 us -> 228 us  [per_device(): piece = lax.all_gather(env_blocks, 'term', axis=0, tiled=True)]
    all_gather x1 -> x0, waiting for transfers between devices: 57.5 us -> none  [per_device(): core_full = lax.all_gather(core_blocks, 'term', axis=1, tiled=True)]
    all_to_all x0 -> x1, starting transfers between devices: none -> 12.3 us  [_draw_threads(): res = lax.all_to_all(h_now, 'term', 0, 0)]
    another operation x0 -> x1, local copies, waits for them, and re-layouts: none -> 5.12 us  [_draw_threads(): h_now = jnp.stack(everything)]
    unnamed x11 -> x13, local copies, waits for them, and re-layouts: 9.72 us -> 9.68 us
  transfers between devices with their start and end apart: 2 -> 2, of which waited for: 2 -> 1; matrix products, arithmetic and copies ran while one was open for 14% -> 12% of each run, Pallas kernels for 0% -> 0%
where the time goes in v1:
time: 409 us; the launch traced here: 408 us
  waiting for transfers between devices  229 us (56%)
  blocking collectives  55.5 us (14%)
  local copies, waits for them, and re-layouts  52.3 us (13%)
  matrix products  41.7 us (10%)
  between operations  13.5 us (3%)
  starting transfers between devices  12.3 us (3%)
    all_gather x1, waiting for transfers between devices, per_device(): piece = lax.all_gather(env_blocks, 'term', axis=0, tiled=True)  228 us
    all_to_all x1, blocking collectives, sum_at_owner(): pieces = lax.all_to_all(split_up(array, dim, peers), axis, 0, 0, tiled=True)  55.5 us
    reshape x1, local copies, waits for them, and re-layouts, per_device(): flat = piece.reshape(count, nb_local, blk * blk)  19.7 us
    reshape x1, local copies, waits for them, and re-layouts, per_device(): pair_terms = pair_terms.reshape(pairs_local, blk * blk)  14.5 us
    dot_general x1, matrix products, per_device(): jnp.einsum('wpi,wix->px', weights, flat, preferred_element_type=jnp.float32)  13.2 us
    all_to_all x1, starting transfers between devices, _draw_threads(): res = lax.all_to_all(h_now, 'term', 0, 0)  12.3 us
    dot_general x1, matrix products, per_device(): jnp.einsum('prc,prd->pcd', masked, half, preferred_element_type=jnp.float32)  11.7 us
    unnamed x13, local copies, waits for them, and re-layouts  9.68 us
  transfers between devices with their start and end apart: 2, of which 1 were waited for; matrix products, arithmetic and copies ran while one was open for 12% of the time, Pallas kernels for 0%

profile of v1, /device:TPU:1, one launch (start us, length us, event | category | flops | bytes accessed | tf_op | source)
XLA Modules:
  0.0 407.8 jit_solution(15184691210779697362)
XLA Ops:
  6.5 0.0 copy-start
  6.5 0.0 all-gather.2.cloned.1.call-start
  6.5 0.7 all-gather.2.cloned.1.call-update
  7.3 5.1 %stack.2 = bf16[32,64,8,256]{3,2,1,0:T(8,128)(2,1)} broadcast(bf16[64,8,256]{2,1,0:T(8,128)(2,1)} %param.7), dimensions={1,2,3} | broadcast | bytes 8650752 | tf_op jit(solution)/shard_map/stack | solution.py:9
  12.4 0.0 copy-start.4
  12.4 0.0 copy-start.2
  12.4 0.0 copy-start.3
  12.4 12.3 %all-to-all-start = ((bf16[32,64,8,256]{3,2,1,0:T(8,128)(2,1)}), bf16[32,64,8,256]{3,2,1,0:T(8,128)(2,1)}, u32[]{:S(2)}, u32[]{:S(2)}) async-start(bf16[32,64,8,256]{3,2,1,0:T(8,128)(2,1)} %stack.2), calls=%async_computation | async-start | bytes 16777216 | tf_op jit(solution)/shard_map/all_to_all | solution.py:10
  24.7 0.0 copy-done
  24.8 0.0 copy-done.4
  24.8 0.0 copy-done.2
  24.8 0.0 copy-done.3
  24.8 0.1 select_reduce_fusion.1
  24.9 0.1 iota_compare_fusion
  25.0 227.9 %all-gather.2.cloned.1.call-done = bf16[32,2,256,256]{3,2,1,0:T(8,128)(2,1)} async-done(((bf16[1,2,256,256]{3,2,1,0:T(8,128)(2,1)}), bf16[32,2,256,256]{3,2,1,0:T(8,128)(2,1)}) %all-gather.2.cloned.1.call-update) | async-done | bytes 8388624 | tf_op jit(solution)/shard_map/all_gather | solution.py:47
  252.9 19.7 %reshape.116 = bf16[32,2,65536]{2,1,0:T(2,128)(2,1)} reshape(bf16[32,2,256,256]{3,2,1,0:T(8,128)(2,1)} %all-gather.2.cloned.1.call-done) | data formatting | bytes 16777216 | tf_op jit(solution)/shard_map/reshape | solution.py:50
  272.6 13.2 %fusion = bf16[64,65536]{1,0:T(8,128)(2,1)} fusion(bf16[32,2,65536]{2,1,0:T(2,128)(2,1)} %reshape.116, bf16[64,2]{0,1:T(2,128)(2,1)S(1)} %compare_convert_fusion, bf16[32,64]{1,0:T(8,128)(2,1)S(1)} %bitcast.39), kind=kOutput, calls=%fused_computation.1 | convolution fusion | flops 541069312 | bytes 16781568 | tf_op jit(solution)/shard_map/wpi,wix->px/dot_general | solution.py:51
  285.8 8.8 %copy.25 = bf16[8,8,256,256]{3,2,1,0:T(8,128)(2,1)} copy(bf16[8,8,256,256]{3,1,2,0:T(8,128)(2,1)} %bitcast.36) | data formatting | bytes 16777216
  294.6 0.0 all-to-all-done
  294.6 7.6 %fusion.30 = bf16[64,256,256]{2,1,0:T(8,128)(2,1)S(1)} fusion(bf16[64,256,256]{2,1,0:T(8,128)(2,1)} %bitcast.37, bf16[32,64,8,256]{3,2,1,0:T(8,128)(2,1)} %all-to-all-done, pred[64,256]{1,0:T(8,128)(4,1)S(1)} %get-tuple-element.7, pred[64,256]{1,0:T(8,128)(4,1)S(1)} %get-tuple-element.8), kind=kOutput, calls=%fused_computation.5.clone.2 | convolution fusion | flops 2160066560 | bytes 25198592 | tf_op jit(solution)/shard_map/prc,pcd->prd/dot_general | solution.py:53
  302.2 11.7 %fusion.2 = f32[64,256,256]{2,1,0:T(8,128)} fusion(bf16[32,64,8,256]{3,2,1,0:T(8,128)(2,1)} %all-to-all-done, pred[64,256]{1,0:T(8,128)(4,1)S(1)} %get-tuple-element.7, pred[64,256]{1,0:T(8,128)(4,1)S(1)} %get-tuple-element.8, bf16[64,256,256]{2,1,0:T(8,128)(2,1)S(1)} %fusion.30), kind=kOutput, calls=%fused_computation.4 | convolution fusion | flops 2155872256 | bytes 33587200 | tf_op jit(solution)/shard_map/prc,prd->pcd/dot_general | solution.py:56
  313.9 14.5 %reshape.115 = f32[64,65536,1]{1,0,2:T(8,128)} reshape(f32[64,256,256]{2,1,0:T(8,128)} %fusion.2) | data formatting | bytes 33554432 | tf_op jit(solution)/shard_map/reshape | solution.py:57
  328.5 9.2 %fusion.15 = f32[8,2,65536]{2,0,1:T(8,128)S(1)} fusion(f32[64,65536,1]{1,0,2:T(8,128)} %reshape.115, s32[8,2]{0,1:T(2,128)S(1)} %multiply_add_fusion, s32[64]{0:T(128)S(1)} %copy-done.2), kind=kOutput, calls=%fused_computation.21 | convolution fusion | flops 805307392 | bytes 20971840 | tf_op jit(solution)/shard_map/dot_general | solution.py:60
  337.6 0.0 copy-start.1
  337.6 3.2 copy.21
  340.9 55.5 %all_to_all.10 = f32[8,2,65536]{2,1,0:T(2,128)} all-to-all(f32[8,2,65536]{2,1,0:T(2,128)S(1)} %copy.21), channel_id=1, replica_groups=mesh['sec'=8,'term'=32] {'sec'}, dimensions={0} | all-to-all | bytes 8388608 | tf_op jit(solution)/shard_map/all_to_all | solution.py:21
  396.4 3.7 reduce_sum.29
  400.1 0.8 copy.41
  401.0 0.0 copy-done.1
  (5 shorter events, 0.0 us)
Async XLA Ops:
  6.5 18.1 %copy-start = (bf16[32,32,64]{2,1,0:T(8,128)(2,1)S(1)}, bf16[32,32,64]{2,1,0:T(8,128)(2,1)}, u32[]{:S(2)}) copy-start(bf16[32,32,64]{2,1,0:T(8,128)(2,1)} %param.8) | copy-start | bytes 393220
  6.5 246.3 %all-gather.2.cloned.1.call-start = ((), (), s32[]{:S(2)}) async-start(), calls=%async_computation.2 | async-start | bytes 8650752 | tf_op jit(solution)/shard_map/all_gather | solution.py:47
  12.4 12.4 %copy-start.4 = (s32[64]{0:T(128)S(1)}, s32[64]{0:T(128)}, u32[]{:S(2)}) copy-start(s32[64]{0:T(128)} %param.9) | copy-start | bytes 772
  12.4 12.4 %copy-start.2 = (s32[64]{0:T(128)S(1)}, s32[64]{0:T(128)}, u32[]{:S(2)}) copy-start(s32[64]{0:T(128)} %param.10) | copy-start | bytes 772
  12.4 12.4 %copy-start.3 = (s32[16]{0:T(128)S(1)}, s32[16]{0:T(128)}, u32[]{:S(2)}) copy-start(s32[16]{0:T(128)} %param.11) | copy-start | bytes 196
  12.4 282.2 %all-to-all-start = ((bf16[32,64,8,256]{3,2,1,0:T(8,128)(2,1)}), bf16[32,64,8,256]{3,2,1,0:T(8,128)(2,1)}, u32[]{:S(2)}, u32[]{:S(2)}) async-start(bf16[32,64,8,256]{3,2,1,0:T(8,128)(2,1)} %stack.2), calls=%async_computation | async-start | bytes 16777216 | tf_op jit(solution)/shard_map/all_to_all | solution.py:10
  337.6 63.4 %copy-start.1 = (bf16[32,32,64]{2,1,0:T(8,128)(2,1)S(1)}, bf16[32,32,64]{2,1,0:T(8,128)(2,1)}, u32[]{:S(2)}) copy-start(bf16[32,32,64]{2,1,0:T(8,128)(2,1)} %param.8) | copy-start | bytes 393220
Sparse Core Ops, SparseCore 0:
  9.9 242.9 all-gather.1
